TPU v7x, 32 devices: a whole 2x2x4 slice. The times are simulated.
32 devices in a mesh: rows: 8 (over y, x, core), rhs: 4 (over z).
Axes of the slice: x: 2, y: 2, z: 4, core: 2. Of those that a mesh axis runs over, the one named last changes fastest.
Arguments:
- samples: float32 [65536, 16], P(('rows', 'rhs')), may hold values from -5 to 5
- freq_table: float32 [4096, 16], replicated, may hold values from -3 to 3
- feature_seeds: int32 [512], replicated, may hold values from 0 to 4095
- phases: float32 [512], replicated, may hold values from -3.140625 to 3.140625
- treatment_features: bfloat16 [65536, 512], P('rows', 'rhs'), may hold values from -2.5 to 2.5, as said below
Outputs:
- coefficients: float32 [512, 512], replicated
- fitted: float32 [65536, 512], P(('rows', 'rhs'))
Inputs may be any that keep to these rules, and one draw needn't show every extreme that they name: `treatment_features`: treatment features depend on the instrument values.
All inputs are finite; a program needn't handle non-finite values.
Results may differ from a plain program's by a relative error of at most 0.0008.
The roundings to bfloat16 on the way count: a program that leaves them out, or rounds other values in their place, can miss the bound.
Values may be sent and summed in bfloat16 or wider, within the bound.
A program may use at most 64 MiB of HBM per device.

v0:
```python
import jax
import jax.numpy as jnp
from jax import lax
from jax.sharding import PartitionSpec as P

ridge = 0.05


def solve_with(factor, right):
    lower = lax.linalg.triangular_solve(factor, right, left_side=True, lower=True)
    return lax.linalg.triangular_solve(factor, lower, left_side=True, lower=True, transpose_a=True)


def features_of(values, freqs, phases):
    angles = (
        jnp.dot(
            values, freqs.T, precision=lax.Precision.HIGHEST, preferred_element_type=jnp.float32
        )
        + phases
    )
    return (jnp.sqrt(jnp.float32(2.0)) * jnp.cos(angles)).astype(jnp.bfloat16)


def body(samples, freq_table, feature_seeds, phases, treatment_features):
    own_rows = samples.shape[0]
    count = own_rows * lax.axis_size("rows") * lax.axis_size("rhs")
    freqs = freq_table[feature_seeds]
    contract = (((0,), (0,)), ((), ()))
    instruments = features_of(samples, freqs, phases)
    gram_part = lax.dot_general(
        instruments, instruments, contract, preferred_element_type=jnp.float32
    )
    gram = lax.psum(gram_part, ("rows", "rhs")) / count
    gram = gram + ridge * jnp.eye(gram.shape[0], dtype=jnp.float32)
    factor = jnp.linalg.cholesky(gram)
    targets = lax.all_to_all(treatment_features, "rhs", split_axis=0, concat_axis=1, tiled=True)
    cross_part = lax.dot_general(instruments, targets, contract, preferred_element_type=jnp.float32)
    cross = lax.psum(cross_part, ("rows", "rhs")) / count
    coefficients = solve_with(factor, cross)
    fitted = jnp.dot(
        instruments, coefficients.astype(jnp.bfloat16), preferred_element_type=jnp.float32
    )
    return (coefficients, fitted)


def solution(mesh):
    placed = (P(("rows", "rhs"), None), P(), P(), P(), P("rows", "rhs"))
    return jax.shard_map(
        body, mesh=mesh, in_specs=placed, out_specs=(P(), P(("rows", "rhs"), None)), check_vma=False
    )
```

profile of v0, /device:TPU:0, one launch (start us, length us, event | category | flops | bytes accessed | tf_op | source)
XLA Modules:
  0.0 364.8 jit_solution(18324534306063840201)
XLA Ops:
  7.2 6.5 %all-to-all-start = ((bf16[4,2048,128]{2,1,0:T(8,128)(2,1)}), bf16[4,2048,128]{2,1,0:T(8,128)(2,1)S(1)}, u32[]{:S(2)}, u32[]{:S(2)}) async-start(bf16[4,2048,128]{2,1,0:T(8,128)(2,1)} %bitcast.66), calls=%async_computation | async-start | bytes 4194304 | tf_op jit(solution)/shard_map/all_to_all | solution.py:36
  13.7 1.9 copy.31
  15.7 2.6 gather_fusion
  18.3 17.9 %multiply_convert_fusion = bf16[512,2048]{1,0:T(8,128)(2,1)S(1)} fusion(f32[512,16]{1,0:T(8,128)S(1)} %gather_fusion, f32[2048,16]{0,1:T(8,128)S(1)} %copy-done, f32[512]{0:T(512)S(1)} %copy-done.8), kind=kOutput, calls=%fused_computation.3 | convolution fusion | flops 204472320 | bytes 2263040 | tf_op jit(solution)/shard_map/dot_general | solution.py:16
  36.3 1.3 copy-done.3
  37.6 2.3 fusion.50
  39.8 22.0 %all-to-all-done = bf16[4,2048,128]{2,1,0:T(8,128)(2,1)S(1)} async-done(((bf16[4,2048,128]{2,1,0:T(8,128)(2,1)}), bf16[4,2048,128]{2,1,0:T(8,128)(2,1)S(1)}, u32[]{:S(2)}, u32[]{:S(2)}) %all-to-all-start) | async-done | bytes 2097184 | tf_op jit(solution)/shard_map/all_to_all | solution.py:36
  61.9 3.1 copy.42
  65.0 4.5 %fusion.51 = f32[512,512]{0,1:T(8,128)} fusion(bf16[512,2048]{1,0:T(8,128)(2,1)} %copy-done.3, bf16[2048,512]{0,1:T(8,128)(2,1)} %bitcast.67), kind=kOutput, calls=%fused_computation.97 | convolution fusion | flops 1073741824 | bytes 5242880 | tf_op jit(solution)/shard_map/dot_general | solution.py:37
  69.5 133.9 %all-reduce.4.cloned.1.call-done = (f32[512,512]{0,1:T(8,128)}, f32[512,512]{0,1:T(8,128)}) async-done(((f32[512,512]{0,1:T(8,128)}, f32[512,512]{0,1:T(8,128)}), (f32[512,512]{0,1:T(8,128)}, f32[512,512]{0,1:T(8,128)})) %all-reduce.4.cloned.1.call-update) | async-done | bytes 2097168 | tf_op jit(solution)/shard_map/psum | solution.py:38
  203.4 2.8 select_add_fusion
  206.2 1.6 copy.33
  208.1 1.0 copy-done.5
  209.1 11.7 %cholesky.103 = f32[128,128]{1,0:T(8,128)S(1)} custom-call(f32[128,128]{1,0:T(8,128)S(1)} %cholesky.263), custom_call_target="Cholesky" | custom-call | tf_op jit(solution)/shard_map/jit(cholesky)/cholesky | solution.py:35
  220.9 9.8 %custom-call.32 = f32[1,128,128]{1,2,0:T(8,128)S(1)} custom-call(f32[1,128,128]{2,1,0:T(8,128)S(1)} %get-tuple-element.39), custom_call_target="InvertDiagBlocksLowerTriangular" | custom-call | tf_op jit(solution)/shard_map/jit(cholesky)/cholesky | solution.py:35
  230.7 1.2 fusion.25
  232.0 1.3 convolution_subtract_fusion.6
  233.4 11.9 %cholesky.215 = f32[128,128]{1,0:T(8,128)S(1)} custom-call(f32[128,128]{1,0:T(8,128)S(1)} %cholesky.267), custom_call_target="Cholesky" | custom-call | tf_op jit(solution)/shard_map/jit(cholesky)/cholesky | solution.py:35
  245.4 9.8 %custom-call.33 = f32[1,128,128]{1,2,0:T(8,128)S(1)} custom-call(f32[1,128,128]{2,1,0:T(8,128)S(1)} %get-tuple-element.37), custom_call_target="InvertDiagBlocksLowerTriangular" | custom-call | tf_op jit(solution)/shard_map/jit(cholesky)/cholesky | solution.py:35
  255.7 1.5 convolution_subtract_fusion.7
  257.2 11.7 %cholesky.236 = f32[128,128]{1,0:T(8,128)S(1)} custom-call(f32[128,128]{1,0:T(8,128)S(1)} %cholesky.272), custom_call_target="Cholesky" | custom-call | tf_op jit(solution)/shard_map/jit(cholesky)/cholesky | solution.py:35
  269.1 9.8 %custom-call.34 = f32[1,128,128]{1,2,0:T(8,128)S(1)} custom-call(f32[1,128,128]{2,1,0:T(8,128)S(1)} %get-tuple-element.35), custom_call_target="InvertDiagBlocksLowerTriangular" | custom-call | tf_op jit(solution)/shard_map/jit(cholesky)/cholesky | solution.py:35
  279.2 1.3 convolution_subtract_fusion.8
  280.5 11.9 %cholesky.253 = f32[128,128]{1,0:T(8,128)S(1)} custom-call(f32[128,128]{1,0:T(8,128)S(1)} %convolution_subtract_fusion.8), custom_call_target="Cholesky" | custom-call | tf_op jit(solution)/shard_map/jit(cholesky)/cholesky | solution.py:35
  292.6 0.6 compare_reduce_fusion.3
  293.2 0.7 compare_reduce_fusion.2
  293.9 0.6 compare_reduce_fusion.1
  294.5 0.7 compare_reduce_fusion
  297.9 8.9 %while.1 = (s32[]{:T(128)}, f32[512,512]{0,1:T(8,128)S(1)}, s32[4,2]{0,1:T(2,128)S(1)}, f32[4,128,128]{2,1,0:T(8,128)S(1)}, s32[]{:T(128)}) while((s32[]{:T(128)}, f32[512,512]{0,1:T(8,128)S(1)}, s32[4,2]{0,1:T(2,128)S(1)}, f32[4,128,128]{2,1,0:T(8,128)S(1)}, s32[]{:T(128)}) %tuple.30), condition=%wide.while_cond, body=%wide.while_body.sunk | while | flops 2 | bytes 393329 | solution.py:11
  298.0 0.6 fusion.70
  298.6 1.4 dynamic-slice.7
  300.2 0.6 fusion.70
  300.8 1.4 dynamic-slice.7
  302.4 0.6 fusion.70
  303.0 1.4 dynamic-slice.7
  304.7 0.6 fusion.70
  305.3 1.4 dynamic-slice.7
  306.8 39.3 %custom-call.35 = f32[4,128,128]{1,2,0:T(8,128)S(1)} custom-call(f32[4,128,128]{2,1,0:T(8,128)S(1)} %get-tuple-element.9), custom_call_target="InvertDiagBlocksLowerTriangular" | custom-call | tf_op jit(solution)/shard_map/triangular_solve | solution.py:11
  346.1 0.4 fusion.19
  346.6 0.6 convolution_subtract_fusion.3
  347.2 0.4 fusion.40
  347.6 1.0 convolution_subtract_fusion.2
  349.0 1.5 convolution_subtract_fusion.5
  350.5 0.4 fusion.44
  352.0 0.4 convolution_subtract_fusion
  352.8 0.6 convolution_subtract_fusion.4
  353.9 0.5 copy-done.4
  354.4 3.3 fusion.17
  (62 shorter events, 4.9 us)
Async XLA Ops:
  7.2 11.2 %copy-start = (f32[2048,16]{0,1:T(8,128)S(1)}, f32[2048,16]{0,1:T(8,128)}, u32[]{:S(2)}) copy-start(f32[2048,16]{0,1:T(8,128)} %param.5) | copy-start | bytes 393220
  7.2 6.6 %copy-start.6 = (f32[4096,16]{0,1:T(8,128)S(1)}, f32[4096,16]{0,1:T(8,128)}, u32[]{:S(2)}) copy-start(f32[4096,16]{0,1:T(8,128)} %param.6) | copy-start | bytes 786436
  7.2 54.7 %all-to-all-start = ((bf16[4,2048,128]{2,1,0:T(8,128)(2,1)}), bf16[4,2048,128]{2,1,0:T(8,128)(2,1)S(1)}, u32[]{:S(2)}, u32[]{:S(2)}) async-start(bf16[4,2048,128]{2,1,0:T(8,128)(2,1)} %bitcast.66), calls=%async_computation | async-start | bytes 4194304 | tf_op jit(solution)/shard_map/all_to_all | solution.py:36
  13.7 2.0 copy-start.7
  13.7 4.6 %copy-start.8 = (f32[512]{0:T(512)S(1)}, f32[512]{0:T(512)}, u32[]{:S(2)}) copy-start(f32[512]{0:T(512)} %param.8) | copy-start | bytes 6148
  13.7 189.7 %all-reduce.4.cloned.1.call-start = ((), (), s32[]{:S(2)}) async-start(), calls=%async_computation.1 | async-start | bytes 4194304 | tf_op jit(solution)/shard_map/psum | solution.py:38
  36.2 1.3 copy-start.3
  206.2 1.7 copy-start.2
  208.1 1.0 copy-start.5
  352.8 1.6 copy-start.4
  354.4 3.3 copy-start.1
Sparse Core Ops, SparseCore 0:
  69.6 133.7 all-reduce.3
where the time goes:
time: 369 us; the launch traced here: 365 us
  waiting for transfers between devices  156 us (42%)
  other arithmetic  122 us (33%)
  matrix products  41.5 us (11%)
  local copies, waits for them, and re-layouts  21.6 us (6%)
  between operations  17.2 us (5%)
  starting transfers between devices  6.53 us (2%)
    psum x1, waiting for transfers between devices, body(): cross = lax.psum(cross_part, ('rows', 'rhs')) / count  134 us
    another operation x15, other arithmetic, body(): factor = jnp.linalg.cholesky(gram)  79.4 us
    another operation x4, other arithmetic, solve_with(): lax.linalg.triangular_solve(factor, lower, left_side=True, lower=True, tr...  39.5 us
    all_to_all x1, waiting for transfers between devices, body(): lax.all_to_all(treatment_features, 'rhs', split_axis=0, concat_axis=1, ti...  22 us
    dot_general x1, matrix products, features_of(): jnp.dot(values, freqs.T, precision=lax.Precision.HIGHEST, preferred_eleme...  17.9 us
    another operation x20, local copies, waits for them, and re-layouts  8.79 us
  transfers between devices with their start and end apart: 2, of which 2 were waited for; matrix products, arithmetic and copies ran while one was open for 7% of the time, Pallas kernels for 0%

commit v1 on v0

--- a/solution.py
+++ b/solution.py
@@ -33,7 +33,10 @@
     gram = lax.psum(gram_part, ("rows", "rhs")) / count
     gram = gram + ridge * jnp.eye(gram.shape[0], dtype=jnp.float32)
     factor = jnp.linalg.cholesky(gram)
-    targets = lax.all_to_all(treatment_features, "rhs", split_axis=0, concat_axis=1, tiled=True)
+    size = lax.axis_size("rhs")
+    shards = jnp.stack(jnp.split(treatment_features, size, axis=0), axis=0)
+    shards = lax.all_to_all(shards, "rhs", split_axis=0, concat_axis=0)
+    targets = jnp.concatenate(shards, axis=1)
     cross_part = lax.dot_general(instruments, targets, contract, preferred_element_type=jnp.float32)
     cross = lax.psum(cross_part, ("rows", "rhs")) / count
     coefficients = solve_with(factor, cross)

time: 369 us -> 369 us (level)
  local copies, waits for them, and re-layouts: 21.6 us -> 16.2 us
  waiting for transfers between devices: 156 us -> 160 us
    all_to_all x1, waiting for transfers between devices: 22 us -> 25.9 us  [body(): shards = lax.all_to_all(shards, 'rhs', split_axis=0, concat_axis=0)]
  transfers between devices with their start and end apart: 2 -> 2, of which waited for: 2 -> 2; matrix products, arithmetic and copies ran while one was open for 7% -> 6% of each run, Pallas kernels for 0% -> 0%
where the time goes in v1:
time: 369 us; the launch traced here: 365 us
  waiting for transfers between devices  160 us (43%)
  other arithmetic  123 us (33%)
  matrix products  41.3 us (11%)
  between operations  17.2 us (5%)
  local copies, waits for them, and re-layouts  16.2 us (4%)
  starting transfers between devices  6.51 us (2%)
    psum x1, waiting for transfers between devices, body(): cross = lax.psum(cross_part, ('rows', 'rhs')) / count  134 us
    another operation x15, other arithmetic, body(): factor = jnp.linalg.cholesky(gram)  79.4 us
    another operation x4, other arithmetic, solve_with(): lax.linalg.triangular_solve(factor, lower, left_side=True, lower=True, tr...  39.5 us
    all_to_all x1, waiting for transfers between devices, body(): shards = lax.all_to_all(shards, 'rhs', split_axis=0, concat_axis=0)  25.9 us
    dot_general x1, matrix products, features_of(): jnp.dot(values, freqs.T, precision=lax.Precision.HIGHEST, preferred_eleme...  18.4 us
    another operation x20, local copies, waits for them, and re-layouts  8.21 us
  transfers between devices with their start and end apart: 2, of which 2 were waited for; matrix products, arithmetic and copies ran while one was open for 6% of the time, Pallas kernels for 0%

profile of v1, /device:TPU:0, one launch (start us, length us, event | category | flops | bytes accessed | tf_op | source)
XLA Modules:
  0.0 364.7 jit_solution(5109882198727694644)
XLA Ops:
  7.2 1.7 fusion.50
  9.8 1.6 pad_maximum_fusion
  11.4 6.5 %all-to-all-start = ((bf16[4,2048,128]{1,2,0:T(8,128)(2,1)}), bf16[4,2048,128]{1,2,0:T(8,128)(2,1)}, u32[]{:S(2)}, u32[]{:S(2)}) async-start(bf16[4,2048,128]{1,2,0:T(8,128)(2,1)} %pad_maximum_fusion), calls=%async_computation | async-start | bytes 4194304 | tf_op jit(solution)/shard_map/all_to_all | solution.py:38
  17.9 0.6 copy.19
  18.5 1.0 gather_fusion
  19.6 18.4 %multiply_convert_fusion = bf16[512,2048]{1,0:T(8,128)(2,1)S(1)} fusion(f32[512,16]{1,0:T(8,128)S(1)} %gather_fusion, f32[2048,16]{0,1:T(8,128)S(1)} %copy-done, f32[512]{0:T(512)S(1)} %copy-done.8), kind=kOutput, calls=%fused_computation.3 | convolution fusion | flops 204472320 | bytes 2263040 | tf_op jit(solution)/shard_map/dot_general | solution.py:16
  38.0 2.3 fusion.51
  40.3 25.9 %all-to-all-done = bf16[4,2048,128]{1,2,0:T(8,128)(2,1)} async-done(((bf16[4,2048,128]{1,2,0:T(8,128)(2,1)}), bf16[4,2048,128]{1,2,0:T(8,128)(2,1)}, u32[]{:S(2)}, u32[]{:S(2)}) %all-to-all-start) | async-done | bytes 2097184 | tf_op jit(solution)/shard_map/all_to_all | solution.py:38
  66.1 3.8 %fusion.52 = f32[512,512]{0,1:T(8,128)} fusion(bf16[512,2048]{1,0:T(8,128)(2,1)S(1)} %multiply_convert_fusion, bf16[2048,512]{0,1:T(8,128)(2,1)} %bitcast.13), kind=kOutput, calls=%fused_computation.99 | convolution fusion | flops 1073741824 | bytes 5242880 | tf_op jit(solution)/shard_map/dot_general | solution.py:40
  70.0 133.9 %all-reduce.4.cloned.1.call-done = (f32[512,512]{0,1:T(8,128)}, f32[512,512]{0,1:T(8,128)}) async-done(((f32[512,512]{0,1:T(8,128)}, f32[512,512]{0,1:T(8,128)}), (f32[512,512]{0,1:T(8,128)}, f32[512,512]{0,1:T(8,128)})) %all-reduce.4.cloned.1.call-update) | async-done | bytes 2097168 | tf_op jit(solution)/shard_map/psum | solution.py:41
  203.9 2.8 select_add_fusion
  206.7 1.6 copy.21
  208.6 1.0 copy-done.5
  209.5 11.7 %cholesky.103 = f32[128,128]{1,0:T(8,128)S(1)} custom-call(f32[128,128]{1,0:T(8,128)S(1)} %cholesky.263), custom_call_target="Cholesky" | custom-call | tf_op jit(solution)/shard_map/jit(cholesky)/cholesky | solution.py:35
  221.3 9.8 %custom-call.32 = f32[1,128,128]{1,2,0:T(8,128)S(1)} custom-call(f32[1,128,128]{2,1,0:T(8,128)S(1)} %get-tuple-element.39), custom_call_target="InvertDiagBlocksLowerTriangular" | custom-call | tf_op jit(solution)/shard_map/jit(cholesky)/cholesky | solution.py:35
  231.1 1.2 fusion.25
  232.3 1.3 convolution_subtract_fusion.6
  233.6 11.9 %cholesky.215 = f32[128,128]{1,0:T(8,128)S(1)} custom-call(f32[128,128]{1,0:T(8,128)S(1)} %cholesky.267), custom_call_target="Cholesky" | custom-call | tf_op jit(solution)/shard_map/jit(cholesky)/cholesky | solution.py:35
  245.9 9.8 %custom-call.33 = f32[1,128,128]{1,2,0:T(8,128)S(1)} custom-call(f32[1,128,128]{2,1,0:T(8,128)S(1)} %get-tuple-element.37), custom_call_target="InvertDiagBlocksLowerTriangular" | custom-call | tf_op jit(solution)/shard_map/jit(cholesky)/cholesky | solution.py:35
  256.2 1.5 convolution_subtract_fusion.7
  257.7 11.7 %cholesky.236 = f32[128,128]{1,0:T(8,128)S(1)} custom-call(f32[128,128]{1,0:T(8,128)S(1)} %cholesky.272), custom_call_target="Cholesky" | custom-call | tf_op jit(solution)/shard_map/jit(cholesky)/cholesky | solution.py:35
  269.6 9.8 %custom-call.34 = f32[1,128,128]{1,2,0:T(8,128)S(1)} custom-call(f32[1,128,128]{2,1,0:T(8,128)S(1)} %get-tuple-element.35), custom_call_target="InvertDiagBlocksLowerTriangular" | custom-call | tf_op jit(solution)/shard_map/jit(cholesky)/cholesky | solution.py:35
  279.7 1.3 convolution_subtract_fusion.8
  281.0 11.9 %cholesky.253 = f32[128,128]{1,0:T(8,128)S(1)} custom-call(f32[128,128]{1,0:T(8,128)S(1)} %convolution_subtract_fusion.8), custom_call_target="Cholesky" | custom-call | tf_op jit(solution)/shard_map/jit(cholesky)/cholesky | solution.py:35
  293.1 0.6 compare_reduce_fusion.2
  293.7 0.6 compare_reduce_fusion.3
  294.3 0.7 compare_reduce_fusion.1
  295.0 0.6 compare_reduce_fusion
  298.3 8.4 %while.1 = (s32[]{:T(128)}, f32[512,512]{0,1:T(8,128)S(1)}, s32[4,2]{0,1:T(2,128)S(1)}, f32[4,128,128]{2,1,0:T(8,128)S(1)}, s32[]{:T(128)}) while((s32[]{:T(128)}, f32[512,512]{0,1:T(8,128)S(1)}, s32[4,2]{0,1:T(2,128)S(1)}, f32[4,128,128]{2,1,0:T(8,128)S(1)}, s32[]{:T(128)}) %tuple.32), condition=%wide.while_cond, body=%wide.while_body.sunk | while | flops 2 | bytes 393321 | solution.py:11
  298.4 0.5 fusion.71
  298.9 1.4 dynamic-slice.7
  300.5 0.5 fusion.71
  301.0 1.4 dynamic-slice.7
  302.6 0.5 fusion.71
  303.1 1.4 dynamic-slice.7
  304.6 0.5 fusion.71
  305.2 1.4 dynamic-slice.7
  306.7 39.3 %custom-call.35 = f32[4,128,128]{1,2,0:T(8,128)S(1)} custom-call(f32[4,128,128]{2,1,0:T(8,128)S(1)} %get-tuple-element.9), custom_call_target="InvertDiagBlocksLowerTriangular" | custom-call | tf_op jit(solution)/shard_map/triangular_solve | solution.py:11
  346.0 0.4 fusion.19
  346.4 0.6 convolution_subtract_fusion.3
  347.0 0.4 fusion.40
  347.4 1.0 convolution_subtract_fusion.2
  348.9 1.5 convolution_subtract_fusion.5
  350.3 0.4 fusion.44
  351.9 0.4 convolution_subtract_fusion
  352.7 0.6 convolution_subtract_fusion.4
  353.8 0.5 copy-done.4
  354.3 3.3 fusion.17
  (67 shorter events, 5.8 us)
Async XLA Ops:
  7.2 12.4 %copy-start = (f32[2048,16]{0,1:T(8,128)S(1)}, f32[2048,16]{0,1:T(8,128)}, u32[]{:S(2)}) copy-start(f32[2048,16]{0,1:T(8,128)} %param.5) | copy-start | bytes 393220
  11.4 6.5 %copy-start.6 = (f32[4096,16]{0,1:T(8,128)S(1)}, f32[4096,16]{0,1:T(8,128)}, u32[]{:S(2)}) copy-start(f32[4096,16]{0,1:T(8,128)} %param.6) | copy-start | bytes 786436
  11.4 54.8 %all-to-all-start = ((bf16[4,2048,128]{1,2,0:T(8,128)(2,1)}), bf16[4,2048,128]{1,2,0:T(8,128)(2,1)}, u32[]{:S(2)}, u32[]{:S(2)}) async-start(bf16[4,2048,128]{1,2,0:T(8,128)(2,1)} %pad_maximum_fusion), calls=%async_computation | async-start | bytes 4194304 | tf_op jit(solution)/shard_map/all_to_all | solution.py:38
  17.8 0.7 copy-start.7
  17.8 1.8 copy-start.8
  17.8 186.1 %all-reduce.4.cloned.1.call-start = ((), (), s32[]{:S(2)}) async-start(), calls=%async_computation.1 | async-start | bytes 4194304 | tf_op jit(solution)/shard_map/psum | solution.py:41
  38.0 28.1 %copy-start.3 = (bf16[512,2048]{1,0:T(8,128)(2,1)}, bf16[512,2048]{1,0:T(8,128)(2,1)S(1)}, u32[]{:S(2)}) copy-start(bf16[512,2048]{1,0:T(8,128)(2,1)S(1)} %multiply_convert_fusion) | copy-start | bytes 6291460
  206.6 1.7 copy-start.2
  208.6 1.0 copy-start.5
  352.7 1.6 copy-start.4
  354.3 3.3 copy-start.1
Sparse Core Ops, SparseCore 0:
  70.1 133.7 all-reduce.3
